TPU v7x, 256 devices: a whole 4x4x8 slice. The times are simulated.
256 devices in a mesh: cuts: 8 (over z), dev: 32 (over x, y, core).
Axes of the slice: x: 4, y: 4, z: 8, core: 2. Of those that a mesh axis runs over, the one named last changes fastest.
Arguments:
- inputs: bfloat16 [131072, 3072], P(('cuts', 'dev')), may hold values from -6 to 6
- cotangent: bfloat16 [131072, 512], P(('cuts', 'dev')), may hold values from -0.29882812 to 0.29882812
- errors: bfloat16 [256, 3072, 512], P(('cuts', 'dev')), may hold values from -6 to 6
- previous_q: float32 [512, 64], replicated, may hold values from -0.25 to 0.25
Outputs:
- new_errors: bfloat16 [256, 3072, 512], P(('cuts', 'dev'))
- p_hat: float32 [3072, 64], replicated
- q_mean: float32 [512, 64], replicated
All inputs are finite; a program needn't handle non-finite values.
Results may differ from a plain program's by a relative error of at most 0.001.
Values sent between devices are 32-bit elements; how exact they have to be, the bound alone decides.
A program may use at most 64 MiB of HBM per device.

v0:
```python
import jax
import jax.numpy as jnp
from jax import lax
from jax.sharding import PartitionSpec as P

HI = lax.Precision.HIGHEST


def split_up(array, dim, peers):
    lengths = array.shape
    parts = array.reshape(*lengths[:dim], peers, lengths[dim] // peers, *lengths[dim + 1 :])
    return jnp.moveaxis(parts, dim, 0)


def sum_at_owner(array, axis, dim):
    parts = split_up(array, dim, lax.axis_size(axis))
    arrived = lax.all_to_all(parts, axis, split_axis=0, concat_axis=0, tiled=True)
    return arrived.sum(axis=0)


def copy_for_each(array, axis):
    copies = jnp.broadcast_to(array, (lax.axis_size(axis), *array.shape))
    return lax.all_to_all(copies, axis, split_axis=0, concat_axis=0, tiled=True)


def of_everyone(array, axis):
    return copy_for_each(array, axis).sum(axis=0)


def joined_along(parts, dim):
    parts = jnp.moveaxis(parts, 0, dim)
    lengths = parts.shape
    return parts.reshape(*lengths[:dim], lengths[dim] * lengths[dim + 1], *lengths[dim + 2 :])


def collect(array, axis, dim):
    parts = copy_for_each(array, axis)
    return joined_along(parts, dim)


def solve_factor(gram, p_rows):
    lower = jnp.linalg.cholesky(gram)
    return lax.linalg.triangular_solve(lower, p_rows, left_side=False, lower=True, transpose_a=True)


def contract_rows(left, right):
    return lax.dot_general(
        left, right, (((0,), (0,)), ((), ())), precision=HI, preferred_element_type=jnp.float32
    )


def body(inputs, cotangent, errors, previous_q):
    grad = lax.dot_general(
        inputs, cotangent, (((0,), (0,)), ((), ())), preferred_element_type=jnp.float32
    )
    merged = grad + errors[0].astype(jnp.float32)
    devices = lax.axis_size("cuts") * lax.axis_size("dev")
    p_share = sum_at_owner(jnp.dot(merged, previous_q, precision=HI), "dev", 0)
    p_share = of_everyone(p_share, "cuts")
    gram = of_everyone(contract_rows(p_share, p_share), "dev")
    hat_share = solve_factor(gram, p_share)
    p_hat = collect(hat_share, "dev", 0)
    q_share = sum_at_owner(contract_rows(merged, p_hat), "dev", 0)
    q_share = of_everyone(q_share, "cuts")
    q_sum = collect(q_share, "dev", 0)
    q_mean = q_sum / devices
    approx = jnp.dot(p_hat, q_mean.T, precision=HI)
    new_errors = (merged - approx).astype(jnp.bfloat16)[None]
    return (new_errors, p_hat, q_mean)


def solution(mesh):
    in_specs = (
        P(("cuts", "dev"), None),
        P(("cuts", "dev"), None),
        P(("cuts", "dev"), None, None),
        P(),
    )
    out_specs = (P(("cuts", "dev"), None, None), P(), P())
    return jax.shard_map(body, mesh=mesh, in_specs=in_specs, out_specs=out_specs, check_vma=False)
```

profile of v0, /device:TPU:1, one launch (start us, length us, event | category | flops | bytes accessed | tf_op | source)
XLA Modules:
  0.0 195.2 jit_solution(17981432938895239607)
XLA Ops:
  0.6 0.0 copy-start
  0.6 4.8 %copy.32 = bf16[1,3072,512]{1,2,0:T(8,128)(2,1)} copy(bf16[1,3072,512]{2,1,0:T(8,128)(2,1)} %param.6) | data formatting | bytes 6291456 | tf_op args[2]
  5.4 0.0 copy-done
  5.4 4.1 %convert_add_fusion = f32[3072,512]{0,1:T(8,128)S(1)} fusion(bf16[512,3072]{1,0:T(8,128)(2,1)S(1)} %copy-done, bf16[512,512]{1,0:T(8,128)(2,1)} %param.5, bf16[1,3072,512]{1,2,0:T(8,128)(2,1)} %copy.32), kind=kOutput, calls=%fused_computation | convolution fusion | flops 1613758464 | bytes 13107200 | tf_op jit(solution)/shard_map/dot_general | solution.py:53
  9.5 2.7 %copy-done.1 = f32[3072,512]{0,1:T(8,128)} copy-done((f32[3072,512]{0,1:T(8,128)}, f32[3072,512]{0,1:T(8,128)S(1)}, u32[]{:S(2)}) %copy-start.1) | copy-done | bytes 6291480
  12.2 5.1 %fusion.5 = f32[3072,64]{0,1:T(8,128)} fusion(f32[3072,512]{0,1:T(8,128)S(1)} %convert_add_fusion, f32[512,64]{0,1:T(8,128)S(1)} %copy-done.2), kind=kOutput, calls=%fused_computation.14 | convolution fusion | flops 1207959552 | bytes 7208960 | tf_op jit(solution)/shard_map/dot_general | solution.py:58
  17.3 2.5 %reshape.29 = f32[32,96,64]{1,0,2:T(8,128)} reshape(f32[3072,64]{0,1:T(8,128)} %fusion.5) | data formatting | bytes 1572864 | tf_op jit(solution)/shard_map/reshape | solution.py:11
  19.8 1.8 copy.33
  21.6 25.4 %all_to_all.35 = f32[32,96,64]{1,2,0:T(8,128)} all-to-all(f32[32,96,64]{1,2,0:T(8,128)S(1)} %copy.33), channel_id=1, replica_groups=mesh['cuts'=8,'dev'=32] {'dev'}, dimensions={0} | all-to-all | bytes 1572864 | tf_op jit(solution)/shard_map/all_to_all | solution.py:17
  47.0 1.3 reduce_sum.45
  48.4 20.3 %all_to_all.36 = f32[8,96,64]{1,2,0:T(8,128)S(1)} all-to-all(f32[8,96,64]{1,2,0:T(8,128)S(1)} %broadcast_in_dim.20), channel_id=1, replica_groups=mesh['cuts'=8,'dev'=32] {'cuts'}, dimensions={0} | all-to-all | bytes 393216 | tf_op jit(solution)/shard_map/all_to_all | solution.py:23
  68.7 0.2 fusion.6
  68.9 1.1 broadcast_in_dim.21
  70.0 2.7 %reshape.34 = f32[32,1,4096]{2,1,0:T(1,128)} reshape(f32[32,64,64]{2,1,0:T(8,128)} %broadcast_in_dim.21) | data formatting | bytes 1048576
  72.6 16.5 %all_to_all.37 = f32[32,1,4096]{2,1,0:T(1,128)} all-to-all(f32[32,1,4096]{2,1,0:T(1,128)} %reshape.34), channel_id=1, replica_groups=mesh['cuts'=8,'dev'=32] {'dev'}, dimensions={0} | all-to-all | bytes 1048576 | tf_op jit(solution)/shard_map/all_to_all | solution.py:23
  89.1 0.6 broadcast.51
  89.7 3.8 %reduce.6 = f32[32,4096]{1,0:T(8,128)} reduce(f32[32,1,4096]{2,1,0:T(1,128)} %all_to_all.37, f32[]{:T(128)} %broadcast.51), dimensions={1}, to_apply=%all_to_all.23.reduce_sub_computation | reduce | bytes 1048580 | tf_op jit(solution)/shard_map/all_to_all | solution.py:23
  93.5 2.4 %reshape.35 = f32[32,64,64]{2,1,0:T(8,128)} reshape(f32[32,4096]{1,0:T(8,128)} %reduce.6) | data formatting | bytes 1048576
  95.9 1.3 reduce_sum.47
  97.2 0.1 copy.35
  97.3 5.8 %cholesky.16 = f32[64,64]{1,0:T(8,128)S(1)} custom-call(f32[64,64]{1,0:T(8,128)S(1)} %fusion.4), custom_call_target="Cholesky" | custom-call | tf_op jit(solution)/shard_map/jit(cholesky)/cholesky | solution.py:42
  103.2 0.6 compare_reduce_fusion
  103.8 0.7 fusion.1
  104.5 4.9 %custom-call.6 = f32[1,64,64]{1,2,0:T(8,128)S(1)} custom-call(f32[1,64,64]{2,1,0:T(8,128)S(1)} %fusion.1), custom_call_target="InvertDiagBlocksLowerTriangular" | custom-call | tf_op jit(solution)/shard_map/triangular_solve | solution.py:43
  109.4 0.3 fusion.2
  109.7 0.1 broadcast_in_dim.22
  109.8 20.3 %all_to_all.38 = f32[32,96,64]{1,2,0:T(8,128)S(1)} all-to-all(f32[32,96,64]{1,2,0:T(8,128)S(1)} %broadcast_in_dim.22), channel_id=1, replica_groups=mesh['cuts'=8,'dev'=32] {'dev'}, dimensions={0} | all-to-all | bytes 1572864 | tf_op jit(solution)/shard_map/all_to_all | solution.py:23
  130.1 1.6 copy.36
  131.7 2.7 %reshape.32 = f32[3072,64,1]{0,1,2:T(8,128)} reshape(f32[32,96,64]{1,0,2:T(8,128)} %copy.36) | data formatting | bytes 1572864 | tf_op jit(solution)/shard_map/reshape | solution.py:33
  134.4 7.3 %fusion.7 = f32[32,16,64]{2,1,0:T(8,128)S(1)} fusion(f32[32,16,3072]{2,1,0:T(8,128)} %bitcast.35, f32[3072,64,1]{0,1,2:T(8,128)} %reshape.32), kind=kOutput, calls=%fused_computation.16 | convolution fusion | flops 1207959552 | bytes 7208960 | tf_op jit(solution)/shard_map/dot_general | solution.py:47
  141.7 0.2 reshape.36
  141.8 11.4 %all_to_all.39 = f32[32,1,1024]{2,1,0:T(1,128)S(1)} all-to-all(f32[32,1,1024]{2,1,0:T(1,128)S(1)} %reshape.36), channel_id=1, replica_groups=mesh['cuts'=8,'dev'=32] {'dev'}, dimensions={0} | all-to-all | bytes 262144 | tf_op jit(solution)/shard_map/all_to_all | solution.py:17
  153.3 1.0 reduce.7
  154.3 0.1 reshape.37
  154.4 0.1 reshape.38
  154.5 9.2 %all_to_all.40 = f32[8,1,1024]{2,1,0:T(1,128)S(1)} all-to-all(f32[8,1,1024]{2,1,0:T(1,128)S(1)} %reshape.38), channel_id=1, replica_groups=mesh['cuts'=8,'dev'=32] {'cuts'}, dimensions={0} | all-to-all | bytes 65536 | tf_op jit(solution)/shard_map/all_to_all | solution.py:23
  163.8 0.8 reduce.8
  164.5 0.1 reshape.39
  164.7 0.8 reshape.40
  165.5 5.1 %all-to-all-start.6 = ((f32[32,1,1024]{2,1,0:T(1,128)}), f32[32,1,1024]{2,1,0:T(1,128)S(1)}, u32[]{:S(2)}, u32[]{:S(2)}) async-start(f32[32,1,1024]{2,1,0:T(1,128)} %reshape.40), calls=%async_computation.6 | async-start | bytes 262144 | tf_op jit(solution)/shard_map/all_to_all | solution.py:23
  170.6 2.7 %reshape.30 = f32[3072,64]{0,1:T(8,128)} reshape(f32[32,96,64]{1,0,2:T(8,128)} %copy.36) | data formatting | bytes 1572864 | tf_op jit(solution)/shard_map/reshape | solution.py:33
  173.3 5.1 %all-to-all-done.6 = f32[32,1,1024]{2,1,0:T(1,128)S(1)} async-done(((f32[32,1,1024]{2,1,0:T(1,128)}), f32[32,1,1024]{2,1,0:T(1,128)S(1)}, u32[]{:S(2)}, u32[]{:S(2)}) %all-to-all-start.6) | async-done | bytes 131104 | tf_op jit(solution)/shard_map/all_to_all | solution.py:23
  178.3 1.0 reduce.9
  179.3 0.8 reshape.41
  180.1 1.0 broadcast_multiply_fusion
  181.1 0.8 copy.39
  181.9 8.7 %fusion = bf16[1,3072,512]{1,2,0:T(8,128)(2,1)} fusion(f32[3072,512]{0,1:T(8,128)} %copy-done.1, f32[3072,64]{0,1:T(8,128)} %reshape.30, f32[512,64]{1,0:T(8,128)S(1)} %bitcast.37), kind=kOutput, calls=%fused_computation.2 | convolution fusion | flops 1211105280 | bytes 10354688 | tf_op jit(solution)/shard_map/dot_general | solution.py:67
  190.6 4.6 %copy.38 = bf16[1,3072,512]{2,1,0:T(8,128)(2,1)} copy(bf16[1,3072,512]{1,2,0:T(8,128)(2,1)} %fusion) | data formatting | bytes 6291456
  (11 shorter events, 0.2 us)
Async XLA Ops:
  0.6 4.8 %copy-start = (bf16[512,3072]{1,0:T(8,128)(2,1)S(1)}, bf16[512,3072]{1,0:T(8,128)(2,1)}, u32[]{:S(2)}) copy-start(bf16[512,3072]{1,0:T(8,128)(2,1)} %param.4) | copy-start | bytes 9437188
  5.4 6.7 %copy-start.2 = (f32[512,64]{0,1:T(8,128)S(1)}, f32[512,64]{0,1:T(8,128)}, u32[]{:S(2)}) copy-start(f32[512,64]{0,1:T(8,128)} %param.7) | copy-start | bytes 393220
  9.5 2.7 %copy-start.1 = (f32[3072,512]{0,1:T(8,128)}, f32[3072,512]{0,1:T(8,128)S(1)}, u32[]{:S(2)}) copy-start(f32[3072,512]{0,1:T(8,128)S(1)} %convert_add_fusion) | copy-start | bytes 18874372
  165.5 12.9 %all-to-all-start.6 = ((f32[32,1,1024]{2,1,0:T(1,128)}), f32[32,1,1024]{2,1,0:T(1,128)S(1)}, u32[]{:S(2)}, u32[]{:S(2)}) async-start(f32[32,1,1024]{2,1,0:T(1,128)} %reshape.40), calls=%async_computation.6 | async-start | bytes 262144 | tf_op jit(solution)/shard_map/all_to_all | solution.py:23
where the time goes:
time: 196 us; the launch traced here: 195 us
  blocking collectives  103 us (53%)
  local copies, waits for them, and re-layouts  33.4 us (17%)
  matrix products  25.6 us (13%)
  other arithmetic  22.3 us (11%)
  starting transfers between devices  5.06 us (3%)
  waiting for transfers between devices  5.06 us (3%)
    all_to_all x4, blocking collectives, copy_for_each(): return lax.all_to_all(copies, axis, split_axis=0, concat_axis=0, tiled=True)  66.3 us
    all_to_all x2, blocking collectives, sum_at_owner(): lax.all_to_all(parts, axis, split_axis=0, concat_axis=0, tiled=True)  36.8 us
    unnamed x17, local copies, waits for them, and re-layouts  20.1 us
    dot_general x1, matrix products, body(): approx = jnp.dot(p_hat, q_mean.T, precision=HI)  8.69 us
    dot_general x2, matrix products, contract_rows(): lax.dot_general(left, right, (((0,), (0,)), ((), ())), precision=HI, pref...  7.46 us
    another operation x3, other arithmetic, solve_factor(): lower = jnp.linalg.cholesky(gram)  6.52 us
    another operation x2, other arithmetic, solve_factor(): lax.linalg.triangular_solve(lower, p_rows, left_side=False, lower=True, t...  5.55 us
    all_to_all x3, other arithmetic, copy_for_each(): return lax.all_to_all(copies, axis, split_axis=0, concat_axis=0, tiled=True)  5.53 us
  transfers between devices with their start and end apart: 1, of which 1 were waited for; matrix products, arithmetic and copies ran while one was open for 1% of the time, Pallas kernels for 0%

commit v1 on v0

v1 whole, which is shorter than its diff:
```python
import functools

import jax
import jax.numpy as jnp
from jax import lax
from jax.experimental import pallas as pl
from jax.experimental.pallas import tpu as pltpu
from jax.sharding import PartitionSpec as P

MESH = pl.DeviceIdType.MESH
F32 = jnp.float32
BF16 = jnp.bfloat16
SUBS = 3


def halves(value):
    high = value.astype(BF16)
    low = (value - high.astype(F32)).astype(BF16)
    return high, low


def mm(left, right, left_dim=1, right_dim=0):
    return lax.dot_general(
        left, right, (((left_dim,), (right_dim,)), ((), ())), preferred_element_type=F32
    )


def kernel(
    nx, ny, nz,
    x_hbm, y_hbm, e_hbm, qt_ref,
    out_ref, phat_ref, qmean_ref,
    xv, ev, yv, merged, m_high, m_low, base,
    part, core_in, chip_sum, plane_in, z_in, full,
    g_own, g_in, gz_in, g_tile, g_full, aug,
    load_sem, core_send, core_recv, rs_send, rs_recv, z_send, z_recv,
    ag_send, ag_recv, fw_send, fw_recv, g_sem,
):
    subs = SUBS
    rank, kvw = qt_ref.shape
    pieces, tok, width = xv.shape
    group = rank // (2 * ny)
    devices = nx * ny * 2 * nz
    z = lax.axis_index("cuts")
    d = lax.axis_index("dev")
    x, y, c = d // (2 * ny), (d // 2) % ny, d % 2

    def at(xx, yy, cc):
        return (z, (xx * ny + yy) * 2 + cc)

    def away(value, step, n):
        return lax.rem(value + step, n)

    partner = at(x, y, 1 - c)

    def remote(src, dst, send, recv, device):
        return pltpu.make_async_remote_copy(
            src_ref=src, dst_ref=dst, send_sem=send, recv_sem=recv, device_id=device, device_id_type=MESH
        )

    def wait_bytes(ref, sem):
        pltpu.make_async_copy(ref, ref, sem).wait()

    x_steps = [(s + nx // 2) % nx for s in range(nx)]
    order = [(s, step) for s in range(subs) for step in [t for t in x_steps if t] + [0]]

    def place(s, step):
        return away(x, step, nx) * subs + s

    y_load = pltpu.make_async_copy(y_hbm, yv, load_sem.at[2, 0])
    y_load.start()
    loads = []
    for i, (s, step) in enumerate(order):
        a = place(s, step)
        start = pl.multiple_of(a * width, width)
        loads.append((
            pltpu.make_async_copy(e_hbm.at[0, pl.ds(start, width), :], ev.at[i], load_sem.at[1, i]),
            pltpu.make_async_copy(x_hbm.at[:, pl.ds(start, width)], xv.at[i], load_sem.at[0, i]),
        ))
        loads[-1][0].start()
        loads[-1][1].start()

    barrier = pltpu.get_barrier_semaphore()
    for k in range(1, 2 * nx * ny):
        pl.semaphore_signal(barrier, inc=1, device_id=(z, away(d, k, 2 * nx * ny)), device_id_type=MESH)
    for k in range(1, nz):
        pl.semaphore_signal(barrier, inc=1, device_id=(away(z, k, nz), d), device_id_type=MESH)

    q_high, q_low = halves(qt_ref[...])
    q_two = jnp.concatenate([q_high, q_low], axis=0)
    y_load.wait()
    t_two = mm(q_two, yv[...], 1, 1)
    t_high, t_low = halves(t_two[:rank] + t_two[rank:])
    base[0:rank, :] = t_high
    base[rank:2 * rank, :] = t_low
    base[2 * rank:4 * rank, :] = q_two

    def left_piece(i):
        for load in loads[i]:
            load.wait()
        both = mm(base[0:2 * rank, :], xv[i]) + mm(base[2 * rank:4 * rank, :], ev[i], 1, 1)
        value = both[:rank] + both[rank:]
        part[i] = value.reshape(2 * ny, group, width)

    def core_copy(i):
        return remote(
            part.at[i, pl.ds((1 - c) * ny, ny)], core_in.at[i], core_send.at[i], core_recv.at[i], partner
        )

    def scatter(i):
        s, step = order[i]
        core_copy(i).wait_recv()
        chip_sum[i] = part[i, pl.ds(c * ny, ny)] + core_in[i]
        for dy in range(ny):
            if step == 0 and dy == 0:
                continue
            slot = ((nx - step) % nx) * ny + (ny - dy) % ny - 1
            yy = away(y, dy, ny)
            remote(
                chip_sum.at[i, yy], plane_in.at[s, slot], rs_send, rs_recv.at[s], at(away(x, step, nx), yy, c)
            ).start()

    def merge_piece(i):
        s, step = order[i]
        a = place(s, step)
        value = mm(xv[i], yv[...], 0, 0) + ev[i].astype(F32)
        merged[a] = value
        high, low = halves(value)
        m_high[a] = high
        m_low[a] = low

    lag = 2
    for i in range(pieces):
        left_piece(i)
        if i == 0:
            pl.semaphore_wait(barrier, 2 * nx * ny - 1 + nz - 1)
        core_copy(i).start()
        if i >= lag:
            scatter(i - lag)
    for i in range(pieces - lag, pieces):
        scatter(i)

    own = [i for i in range(pieces) if order[i][1] == 0]

    def exchange(s):
        wait_bytes(plane_in.at[s], rs_recv.at[s])
        total = chip_sum[own[s], y]
        for slot in range(nx * ny - 1):
            total = total + plane_in[s, slot]
        z_in[s, z] = total
        for k in range(1, nz):
            remote(z_in.at[s, z], z_in.at[s, z], z_send, z_recv.at[s], (away(z, k, nz), d)).start()

    row = c * ny + y

    def spread(s):
        wait_bytes(z_in.at[s, pl.ds(0, nz - 1)], z_recv.at[s])
        total = z_in[s, 0]
        for k in range(1, nz):
            total = total + z_in[s, k]
        a = place(s, 0)
        full[a, row] = total
        for dx in [t for t in x_steps if t] + [0]:
            for dy in range(ny):
                if dx == 0 and dy == 0:
                    continue
                remote(
                    full.at[a, row], full.at[a, row], ag_send, ag_recv.at[s, (nx - dx) % nx],
                    at(away(x, dx, nx), away(y, dy, ny), c),
                ).start()

    half = pieces // 2
    for i in range(half):
        merge_piece(i)
    rest = list(range(half, pieces))
    for s in range(subs):
        exchange(s)
        for i in rest[s * (pieces - half) // subs:(s + 1) * (pieces - half) // subs]:
            merge_piece(i)
    for s in range(subs):
        spread(s)

    near = [0] + [t for t in range(1, nx) if t in (1, nx - 1)] + [t for t in range(2, nx - 1)]
    arrivals = [(s, rx) for s in range(subs) for rx in near]

    def forward(s, rx):
        a = place(s, rx)
        count = ny - 1 if rx == 0 else ny
        wait_bytes(full.at[a, pl.ds(c * ny, count)], ag_recv.at[s, rx])
        mine = full.at[a, pl.ds(c * ny, ny)]
        remote(mine, mine, fw_send, fw_recv.at[s, rx], partner).start()

    def right_piece(s, rx, first):
        a = place(s, rx)
        theirs = full.at[a, pl.ds((1 - c) * ny, ny)]
        wait_bytes(theirs, fw_recv.at[s, rx])
        high, low = halves(full[a].reshape(rank, width))
        two = mm(jnp.concatenate([high, low], axis=0), m_high[a])
        value = two[:rank] + two[rank:] + mm(high, m_low[a])
        if first:
            g_own[...] = value
        else:
            g_own[...] += value

    for i, (s, rx) in enumerate(arrivals):
        forward(s, rx)
        if i >= 1:
            right_piece(*arrivals[i - 1], i == 1)
    right_piece(*arrivals[-1], False)

    g_cols = kvw // nx

    def tile(ref, xx, rr):
        return ref.at[pl.ds(pl.multiple_of(rr * group, group), group), pl.ds(pl.multiple_of(xx * g_cols, g_cols), g_cols)]

    n_dev = 2 * nx * ny
    for k in range(1, n_dev):
        to = away(d, k, n_dev)
        tx, ty, tc = to // (2 * ny), (to // 2) % ny, to % 2
        remote(tile(g_own, tx, tc * ny + ty), g_in.at[n_dev - k - 1], g_sem.at[0], g_sem.at[1], (z, to)).start()

    gram = jnp.zeros((2 * rank, 2 * rank), F32)
    for a in range(pieces):
        high, low = halves(full[a].reshape(rank, width))
        two = jnp.concatenate([high, low], axis=0)
        gram = gram + mm(two, two, 1, 1)
    gram = gram[:rank] + gram[rank:]
    gram = gram[:, :rank] + gram[:, rank:]
    rows = lax.broadcasted_iota(jnp.int32, (rank, 2 * rank), 0)
    lanes = lax.broadcasted_iota(jnp.int32, (rank, 2 * rank), 1)
    aug[:, 0:rank] = gram
    aug[:, rank:2 * rank] = (rows == lanes).astype(F32)[:, :rank]

    def eliminate(k, carry):
        value = aug[...]
        pivot_row = aug[pl.ds(k, 1), :]
        column = jnp.sum(jnp.where(lanes == k, value, 0.0), axis=1, keepdims=True)
        pivot = jnp.sum(jnp.where(lanes[:1] == k, pivot_row, 0.0), axis=1, keepdims=True)
        factor = jnp.where(rows[:, :1] > k, column / pivot, 0.0)
        aug[...] = value - factor * pivot_row
        return carry

    lax.fori_loop(0, rank // 2, eliminate, 0)

    wait_bytes(g_in, g_sem.at[1])
    total = tile(g_own, x, row)[...]
    for k in range(n_dev - 1):
        total = total + g_in[k]
    gz_in[z] = total
    for k in range(1, nz):
        remote(gz_in.at[z], gz_in.at[z], g_sem.at[2], g_sem.at[3], (away(z, k, nz), d)).start()

    lax.fori_loop(rank // 2, rank, eliminate, 0)
    final = aug[...]
    diagonal = jnp.sum(jnp.where(rows == lanes, final, 0.0), axis=1, keepdims=True)
    inverse = final[:, rank:] * (1.0 / jnp.sqrt(diagonal))
    i_high, i_low = halves(inverse)

    wait_bytes(gz_in.at[pl.ds(0, nz - 1)], g_sem.at[3])
    total = gz_in[0]
    for k in range(1, nz):
        total = total + gz_in[k]
    mine = tile(g_full, x, row)
    mine[...] = total
    for k in range(1, n_dev):
        remote(mine, mine, g_sem.at[4], g_sem.at[5], (z, away(d, k, n_dev))).start()

    left = jnp.concatenate([i_high, i_high, i_low], axis=1)

    def applied(value):
        high, low = halves(value)
        return mm(left, jnp.concatenate([high, low, high], axis=0))

    for a in range(pieces):
        value = applied(full[a].reshape(rank, width))
        phat_ref[:, a * width:(a + 1) * width] = value

    wait_bytes(g_in, g_sem.at[5])
    q_mean = applied(g_full[...]) * (1.0 / devices)
    qmean_ref[...] = q_mean
    high, low = halves(q_mean)
    right = jnp.concatenate([high, high, low], axis=0)
    for a in range(pieces):
        high, low = halves(phat_ref[:, a * width:(a + 1) * width])
        value = merged[a] - mm(jnp.concatenate([high, low, high], axis=0), right, 0, 0)
        out_ref[a * width:(a + 1) * width, :] = value.astype(BF16)

    for i in range(pieces):
        core_copy(i).wait_send()
    wait_bytes(plane_in, rs_send)
    wait_bytes(z_in.at[:, pl.ds(0, nz - 1)], z_send)
    wait_bytes(plane_in, ag_send)
    wait_bytes(core_in, fw_send)
    wait_bytes(g_in, g_sem.at[0])
    wait_bytes(gz_in.at[pl.ds(0, nz - 1)], g_sem.at[2])
    wait_bytes(g_in, g_sem.at[4])


def step(nx, ny, nz, inputs, cotangent, errors, previous_q):
    tok, width = inputs.shape
    kvw = cotangent.shape[1]
    rank = previous_q.shape[1]
    subs = SUBS
    pieces = nx * subs
    w = width // pieces
    group = rank // (2 * ny)
    n_dev = 2 * nx * ny
    dma = pltpu.SemaphoreType.DMA
    any_space = pl.BlockSpec(memory_space=pl.ANY)
    vmem = pl.BlockSpec(memory_space=pltpu.VMEM)
    new_errors, p_hat, q_mean = pl.pallas_call(
        functools.partial(kernel, nx, ny, nz),
        out_shape=(
            jax.ShapeDtypeStruct((width, kvw), BF16),
            jax.ShapeDtypeStruct((rank, width), F32),
            jax.ShapeDtypeStruct((rank, kvw), F32),
        ),
        in_specs=[any_space, any_space, any_space, vmem],
        out_specs=(vmem, vmem, vmem),
        scratch_shapes=[
            pltpu.VMEM((pieces, tok, w), BF16),
            pltpu.VMEM((pieces, w, kvw), BF16),
            pltpu.VMEM((tok, kvw), BF16),
            pltpu.VMEM((pieces, w, kvw), F32),
            pltpu.VMEM((pieces, w, kvw), BF16),
            pltpu.VMEM((pieces, w, kvw), BF16),
            pltpu.VMEM((4 * rank, kvw), BF16),
            pltpu.VMEM((pieces, 2 * ny, group, w), F32),
            pltpu.VMEM((pieces, ny, group, w), F32),
            pltpu.VMEM((pieces, ny, group, w), F32),
            pltpu.VMEM((subs, nx * ny - 1, group, w), F32),
            pltpu.VMEM((subs, nz, group, w), F32),
            pltpu.VMEM((pieces, 2 * ny, group, w), F32),
            pltpu.VMEM((rank, kvw), F32),
            pltpu.VMEM((n_dev - 1, group, kvw // nx), F32),
            pltpu.VMEM((nz, group, kvw // nx), F32),
            pltpu.VMEM((group, kvw // nx), F32),
            pltpu.VMEM((rank, kvw), F32),
            pltpu.VMEM((rank, 2 * rank), F32),
            dma((3, pieces)),
            dma((pieces,)),
            dma((pieces,)),
            dma(()),
            dma((subs,)),
            dma(()),
            dma((subs,)),
            dma(()),
            dma((subs, nx)),
            dma(()),
            dma((subs, nx)),
            dma((6,)),
        ],
        compiler_params=pltpu.CompilerParams(
            collective_id=0, has_side_effects=True, vmem_limit_bytes=40 * 2**20
        ),
        name="powersgd",
    )(inputs, cotangent, errors, previous_q.T)
    return new_errors[None], p_hat.T, q_mean.T


def solution(mesh):
    nz = mesh.shape["cuts"]
    side = 1
    while 2 * side * side < mesh.shape["dev"]:
        side *= 2
    in_specs = (
        P(("cuts", "dev"), None),
        P(("cuts", "dev"), None),
        P(("cuts", "dev"), None, None),
        P(),
    )
    out_specs = (P(("cuts", "dev"), None, None), P(), P())
    return jax.shard_map(
        functools.partial(step, side, side, nz), mesh=mesh, in_specs=in_specs, out_specs=out_specs, check_vma=False
    )
```

time: 196 us -> 62 us (0.32)
  blocking collectives: 103 us -> 0 us
  Pallas kernels: 0 us -> 52.2 us
  matrix products: 25.6 us -> 0 us
  local copies, waits for them, and re-layouts: 33.4 us -> 8.92 us
  other arithmetic: 22.3 us -> 0 us
  starting transfers between devices: 5.06 us -> 0 us
  waiting for transfers between devices: 5.06 us -> 0 us
    all_to_all x6 -> x0, blocking collectives: 103 us -> none  [the longest x4 66.3 us: copy_for_each(): return lax.all_to_all(copies, axis, split_axis=0, concat_axis=0, tiled=True)]
    pallas_call x0 -> x1, Pallas kernels: none -> 52.2 us  [step(): pl.pallas_call(functools.partial(kernel, nx, ny, nz), out_shape=(jax.Shap...]
    dot_general x5 -> x0, matrix products: 25.3 us -> none  [the longest x1 8.69 us: body(): approx = jnp.dot(p_hat, q_mean.T, precision=HI)]
    another operation x5 -> x0, other arithmetic: 12.1 us -> none  [the longest x3 6.52 us: solve_factor(): lower = jnp.linalg.cholesky(gram)]
    unnamed x17 -> x11, local copies, waits for them, and re-layouts: 20.1 us -> 8.92 us
    reshape x4 -> x0, local copies, waits for them, and re-layouts: 9.81 us -> none  [the longest x2 5.45 us: joined_along(): parts.reshape(*lengths[:dim], lengths[dim] * lengths[dim + 1], *lengths[d...]
    all_to_all x4 -> x0, other arithmetic: 6.53 us -> none  [the longest x3 5.53 us: copy_for_each(): return lax.all_to_all(copies, axis, split_axis=0, concat_axis=0, tiled=True)]
    all_to_all x1 -> x0, starting transfers between devices: 5.06 us -> none  [copy_for_each(): return lax.all_to_all(copies, axis, split_axis=0, concat_axis=0, tiled=True)]
  transfers between devices with their start and end apart: 1 -> 0, of which waited for: 1 -> 0; matrix products, arithmetic and copies ran while one was open for 1% -> 0% of each run, Pallas kernels for 0% -> 0%
where the time goes in v1:
time: 62 us; the launch traced here: 61.8 us
  Pallas kernels  52.2 us (84%)
  local copies, waits for them, and re-layouts  8.92 us (14%)
  between operations  0.65 us (1%)
    pallas_call x1, Pallas kernels, step(): pl.pallas_call(functools.partial(kernel, nx, ny, nz), out_shape=(jax.Shap...  52.2 us
    unnamed x11, local copies, waits for them, and re-layouts  8.92 us

profile of v1, /device:TPU:1, one launch (start us, length us, event | category | flops | bytes accessed | tf_op | source)
XLA Modules:
  0.0 61.8 jit_solution(13930933453513785965)
XLA Ops:
  0.6 0.0 copy-start
  0.6 1.9 %copy-done = bf16[512,3072]{1,0:T(8,128)(2,1)S(1)} copy-done((bf16[512,3072]{1,0:T(8,128)(2,1)S(1)}, bf16[512,3072]{1,0:T(8,128)(2,1)}, u32[]{:S(2)}) %copy-start) | copy-done | bytes 3145752
  2.5 0.0 copy-start.1
  2.5 1.9 %copy-done.1 = bf16[1,3072,512]{2,1,0:T(8,128)(2,1)S(1)} copy-done((bf16[1,3072,512]{2,1,0:T(8,128)(2,1)S(1)}, bf16[1,3072,512]{2,1,0:T(8,128)(2,1)}, u32[]{:S(2)}) %copy-start.1) | copy-done | bytes 3145752
  4.4 0.0 copy-start.2
  4.4 1.0 %copy-done.2 = bf16[512,512]{1,0:T(8,128)(2,1)S(1)} copy-done((bf16[512,512]{1,0:T(8,128)(2,1)S(1)}, bf16[512,512]{1,0:T(8,128)(2,1)}, u32[]{:S(2)}) %copy-start.2) | copy-done | bytes 524312
  5.5 0.0 copy-start.3
  5.5 0.9 %copy-done.3 = f32[512,64]{0,1:T(8,128)S(1)} copy-done((f32[512,64]{0,1:T(8,128)S(1)}, f32[512,64]{0,1:T(8,128)}, u32[]{:S(2)}) %copy-start.3) | copy-done | bytes 131096
  6.4 52.2 %powersgd.1 = (bf16[3072,512]{1,0:T(8,128)(2,1)S(1)}, f32[64,3072]{1,0:T(8,128)S(1)}, f32[64,512]{1,0:T(8,128)S(1)}) custom-call(bf16[512,3072]{1,0:T(8,128)(2,1)S(1)} %copy-done, bf16[512,512]{1,0:T(8,128)(2,1)S(1)} %copy-done.2, bf16[1,3072,512]{2,1,0:T(8,128)(2,1)S(1)} %copy-done.1, f32[64,512]{1,0:T(8,128)S(1)} %bitcast.6), custom_call_target="tpu_custom_call" | custom-call | tf_op jit(solution)/shard_map/powersgd/pallas_call | solution.py:310
  58.6 1.7 %copy.10 = bf16[1,3072,512]{2,1,0:T(8,128)(2,1)} copy(bf16[1,3072,512]{2,1,0:T(8,128)(2,1)S(1)} %bitcast.4) | data formatting | bytes 6291456
  60.2 0.9 %copy.11 = f32[3072,64]{0,1:T(8,128)} copy(f32[3072,64]{0,1:T(8,128)S(1)} %bitcast.5) | data formatting | bytes 1572864
  61.1 0.7 %copy.12 = f32[512,64]{0,1:T(8,128)} copy(f32[512,64]{0,1:T(8,128)S(1)} %bitcast.7) | data formatting | bytes 262144
Async XLA Ops:
  0.6 1.9 %copy-start = (bf16[512,3072]{1,0:T(8,128)(2,1)S(1)}, bf16[512,3072]{1,0:T(8,128)(2,1)}, u32[]{:S(2)}) copy-start(bf16[512,3072]{1,0:T(8,128)(2,1)} %x_hbm.1) | copy-start | bytes 9437188
  2.5 1.9 %copy-start.1 = (bf16[1,3072,512]{2,1,0:T(8,128)(2,1)S(1)}, bf16[1,3072,512]{2,1,0:T(8,128)(2,1)}, u32[]{:S(2)}) copy-start(bf16[1,3072,512]{2,1,0:T(8,128)(2,1)} %e_hbm.1) | copy-start | bytes 9437188
  4.4 1.0 %copy-start.2 = (bf16[512,512]{1,0:T(8,128)(2,1)S(1)}, bf16[512,512]{1,0:T(8,128)(2,1)}, u32[]{:S(2)}) copy-start(bf16[512,512]{1,0:T(8,128)(2,1)} %y_hbm.1) | copy-start | bytes 1572868
  5.5 0.9 %copy-start.3 = (f32[512,64]{0,1:T(8,128)S(1)}, f32[512,64]{0,1:T(8,128)}, u32[]{:S(2)}) copy-start(f32[512,64]{0,1:T(8,128)} %param.7) | copy-start | bytes 393220

commit v2 on v1

--- a/solution.py
+++ b/solution.py
@@ -10,7 +10,7 @@
 MESH = pl.DeviceIdType.MESH
 F32 = jnp.float32
 BF16 = jnp.bfloat16
-SUBS = 3
+SUBS = 2
 
 
 def halves(value):
@@ -25,13 +25,17 @@
     )
 
 
+def far_first(n):
+    return sorted(range(n), key=lambda step: -min(step, n - step))
+
+
 def kernel(
     nx, ny, nz,
-    x_hbm, y_hbm, e_hbm, qt_ref,
-    out_ref, phat_ref, qmean_ref,
-    xv, ev, yv, merged, m_high, m_low, base,
+    x_hbm, y_hbm, e_hbm, qt_hbm,
+    merged, left_parts, phat_ref, qmean_ref,
+    xv, ev, yv, qt_ref, m_high, m_low, base,
     part, core_in, chip_sum, plane_in, z_in, full,
-    g_own, g_in, gz_in, g_tile, g_full, aug,
+    g_own, g_in, gz_in, g_full, aug,
     load_sem, core_send, core_recv, rs_send, rs_recv, z_send, z_recv,
     ag_send, ag_recv, fw_send, fw_recv, g_sem,
 ):
@@ -60,12 +64,24 @@
     def wait_bytes(ref, sem):
         pltpu.make_async_copy(ref, ref, sem).wait()
 
-    x_steps = [(s + nx // 2) % nx for s in range(nx)]
-    order = [(s, step) for s in range(subs) for step in [t for t in x_steps if t] + [0]]
+    hops = [(dx, dy, dc) for dx in far_first(nx) for dy in far_first(ny) for dc in (0, 1)]
+    hops = sorted([h for h in hops if any(h)], key=lambda h: -min(h[0], nx - h[0]) - min(h[1], ny - h[1]))
+    plane = [(dx, dy) for dx, dy, dc in hops if dc == 0]
+
+    barrier = pltpu.get_barrier_semaphore()
+    for k in far_first(nz):
+        if k:
+            pl.semaphore_signal(barrier, inc=1, device_id=(away(z, k, nz), d), device_id_type=MESH)
+    for dx, dy, dc in hops:
+        pl.semaphore_signal(barrier, inc=1, device_id=at(away(x, dx, nx), away(y, dy, ny), away(c, dc, 2)), device_id_type=MESH)
+
+    order = [(s, step) for s in range(subs) for step in far_first(nx)]
 
     def place(s, step):
         return away(x, step, nx) * subs + s
 
+    q_load = pltpu.make_async_copy(qt_hbm, qt_ref, load_sem.at[2, 1])
+    q_load.start()
     y_load = pltpu.make_async_copy(y_hbm, yv, load_sem.at[2, 0])
     y_load.start()
     loads = []
@@ -79,12 +95,7 @@
         loads[-1][0].start()
         loads[-1][1].start()
 
-    barrier = pltpu.get_barrier_semaphore()
-    for k in range(1, 2 * nx * ny):
-        pl.semaphore_signal(barrier, inc=1, device_id=(z, away(d, k, 2 * nx * ny)), device_id_type=MESH)
-    for k in range(1, nz):
-        pl.semaphore_signal(barrier, inc=1, device_id=(away(z, k, nz), d), device_id_type=MESH)
-
+    q_load.wait()
     q_high, q_low = halves(qt_ref[...])
     q_two = jnp.concatenate([q_high, q_low], axis=0)
     y_load.wait()
@@ -110,7 +121,7 @@
         s, step = order[i]
         core_copy(i).wait_recv()
         chip_sum[i] = part[i, pl.ds(c * ny, ny)] + core_in[i]
-        for dy in range(ny):
+        for dy in far_first(ny):
             if step == 0 and dy == 0:
                 continue
             slot = ((nx - step) % nx) * ny + (ny - dy) % ny - 1
@@ -128,15 +139,15 @@
         m_high[a] = high
         m_low[a] = low
 
-    lag = 2
     for i in range(pieces):
         left_piece(i)
-        if i == 0:
-            pl.semaphore_wait(barrier, 2 * nx * ny - 1 + nz - 1)
+    early = pieces // 2
+    for i in range(early):
+        merge_piece(i)
+    pl.semaphore_wait(barrier, len(hops) + nz - 1)
+    for i in range(pieces):
         core_copy(i).start()
-        if i >= lag:
-            scatter(i - lag)
-    for i in range(pieces - lag, pieces):
+    for i in range(pieces):
         scatter(i)
 
     own = [i for i in range(pieces) if order[i][1] == 0]
@@ -147,7 +158,7 @@
         for slot in range(nx * ny - 1):
             total = total + plane_in[s, slot]
         z_in[s, z] = total
-        for k in range(1, nz):
+        for k in far_first(nz)[:-1]:
             remote(z_in.at[s, z], z_in.at[s, z], z_send, z_recv.at[s], (away(z, k, nz), d)).start()
 
     row = c * ny + y
@@ -159,28 +170,21 @@
             total = total + z_in[s, k]
         a = place(s, 0)
         full[a, row] = total
-        for dx in [t for t in x_steps if t] + [0]:
-            for dy in range(ny):
-                if dx == 0 and dy == 0:
-                    continue
-                remote(
-                    full.at[a, row], full.at[a, row], ag_send, ag_recv.at[s, (nx - dx) % nx],
-                    at(away(x, dx, nx), away(y, dy, ny), c),
-                ).start()
-
-    half = pieces // 2
-    for i in range(half):
-        merge_piece(i)
-    rest = list(range(half, pieces))
+        for dx, dy in plane:
+            remote(
+                full.at[a, row], full.at[a, row], ag_send, ag_recv.at[s, (nx - dx) % nx],
+                at(away(x, dx, nx), away(y, dy, ny), c),
+            ).start()
+
+    rest = list(range(early, pieces))
     for s in range(subs):
         exchange(s)
-        for i in rest[s * (pieces - half) // subs:(s + 1) * (pieces - half) // subs]:
+        for i in rest[s * len(rest) // subs:(s + 1) * len(rest) // subs]:
             merge_piece(i)
     for s in range(subs):
         spread(s)
 
-    near = [0] + [t for t in range(1, nx) if t in (1, nx - 1)] + [t for t in range(2, nx - 1)]
-    arrivals = [(s, rx) for s in range(subs) for rx in near]
+    arrivals = [(s, rx) for s in range(subs) for rx in reversed(far_first(nx))]
 
     def forward(s, rx):
         a = place(s, rx)
@@ -212,11 +216,10 @@
     def tile(ref, xx, rr):
         return ref.at[pl.ds(pl.multiple_of(rr * group, group), group), pl.ds(pl.multiple_of(xx * g_cols, g_cols), g_cols)]
 
-    n_dev = 2 * nx * ny
-    for k in range(1, n_dev):
-        to = away(d, k, n_dev)
-        tx, ty, tc = to // (2 * ny), (to // 2) % ny, to % 2
-        remote(tile(g_own, tx, tc * ny + ty), g_in.at[n_dev - k - 1], g_sem.at[0], g_sem.at[1], (z, to)).start()
+    for dx, dy, dc in hops:
+        tx, ty, tc = away(x, dx, nx), away(y, dy, ny), away(c, dc, 2)
+        slot = ((nx - dx) % nx * ny + (ny - dy) % ny) * 2 + dc - 1
+        remote(tile(g_own, tx, tc * ny + ty), g_in.at[slot], g_sem.at[0], g_sem.at[1], at(tx, ty, tc)).start()
 
     gram = jnp.zeros((2 * rank, 2 * rank), F32)
     for a in range(pieces):
@@ -243,10 +246,10 @@
 
     wait_bytes(g_in, g_sem.at[1])
     total = tile(g_own, x, row)[...]
-    for k in range(n_dev - 1):
+    for k in range(len(hops)):
         total = total + g_in[k]
     gz_in[z] = total
-    for k in range(1, nz):
+    for k in far_first(nz)[:-1]:
         remote(gz_in.at[z], gz_in.at[z], g_sem.at[2], g_sem.at[3], (away(z, k, nz), d)).start()
 
     lax.fori_loop(rank // 2, rank, eliminate, 0)
@@ -261,8 +264,9 @@
         total = total + gz_in[k]
     mine = tile(g_full, x, row)
     mine[...] = total
-    for k in range(1, n_dev):
-        remote(mine, mine, g_sem.at[4], g_sem.at[5], (z, away(d, k, n_dev))).start()
+    for dx, dy, dc in hops:
+        to = at(away(x, dx, nx), away(y, dy, ny), away(c, dc, 2))
+        remote(mine, mine, g_sem.at[4], g_sem.at[5], to).start()
 
     left = jnp.concatenate([i_high, i_high, i_low], axis=1)
 
@@ -273,16 +277,12 @@
     for a in range(pieces):
         value = applied(full[a].reshape(rank, width))
         phat_ref[:, a * width:(a + 1) * width] = value
+        high, low = halves(value)
+        left_parts[a] = jnp.concatenate([high, low, high], axis=0).T
 
     wait_bytes(g_in, g_sem.at[5])
     q_mean = applied(g_full[...]) * (1.0 / devices)
     qmean_ref[...] = q_mean
-    high, low = halves(q_mean)
-    right = jnp.concatenate([high, high, low], axis=0)
-    for a in range(pieces):
-        high, low = halves(phat_ref[:, a * width:(a + 1) * width])
-        value = merged[a] - mm(jnp.concatenate([high, low, high], axis=0), right, 0, 0)
-        out_ref[a * width:(a + 1) * width, :] = value.astype(BF16)
 
     for i in range(pieces):
         core_copy(i).wait_send()
@@ -293,6 +293,25 @@
     wait_bytes(g_in, g_sem.at[0])
     wait_bytes(gz_in.at[pl.ds(0, nz - 1)], g_sem.at[2])
     wait_bytes(g_in, g_sem.at[4])
+
+
+def finish(merged, left_parts, phat_ref, qmean_ref, out_hbm, phat_hbm, qmean_hbm, rows, row_sem, small_sem):
+    pieces, width, kvw = merged.shape
+    small = (
+        pltpu.make_async_copy(phat_ref, phat_hbm, small_sem.at[0]),
+        pltpu.make_async_copy(qmean_ref, qmean_hbm, small_sem.at[1]),
+    )
+    for copy in small:
+        copy.start()
+    high, low = halves(qmean_ref[...])
+    right = jnp.concatenate([high, high, low], axis=0)
+    copies = []
+    for a in range(pieces):
+        rows[a] = (merged[a] - mm(left_parts[a], right)).astype(BF16)
+        copies.append(pltpu.make_async_copy(rows.at[a], out_hbm.at[pl.ds(a * width, width), :], row_sem.at[a]))
+        copies[-1].start()
+    for copy in (*small, *copies):
+        copy.wait()
 
 
 def step(nx, ny, nz, inputs, cotangent, errors, previous_q):
@@ -305,22 +324,23 @@
     group = rank // (2 * ny)
     n_dev = 2 * nx * ny
     dma = pltpu.SemaphoreType.DMA
-    any_space = pl.BlockSpec(memory_space=pl.ANY)
+    hbm = pl.BlockSpec(memory_space=pltpu.HBM)
     vmem = pl.BlockSpec(memory_space=pltpu.VMEM)
-    new_errors, p_hat, q_mean = pl.pallas_call(
+    merged, left_parts, p_hat, q_mean = pl.pallas_call(
         functools.partial(kernel, nx, ny, nz),
         out_shape=(
-            jax.ShapeDtypeStruct((width, kvw), BF16),
+            jax.ShapeDtypeStruct((pieces, w, kvw), F32),
+            jax.ShapeDtypeStruct((pieces, w, 3 * rank), BF16),
             jax.ShapeDtypeStruct((rank, width), F32),
             jax.ShapeDtypeStruct((rank, kvw), F32),
         ),
-        in_specs=[any_space, any_space, any_space, vmem],
-        out_specs=(vmem, vmem, vmem),
+        in_specs=[hbm, hbm, hbm, hbm],
+        out_specs=(vmem, vmem, vmem, vmem),
         scratch_shapes=[
             pltpu.VMEM((pieces, tok, w), BF16),
             pltpu.VMEM((pieces, w, kvw), BF16),
             pltpu.VMEM((tok, kvw), BF16),
-            pltpu.VMEM((pieces, w, kvw), F32),
+            pltpu.VMEM((rank, kvw), F32),
             pltpu.VMEM((pieces, w, kvw), BF16),
             pltpu.VMEM((pieces, w, kvw), BF16),
             pltpu.VMEM((4 * rank, kvw), BF16),
@@ -333,7 +353,6 @@
             pltpu.VMEM((rank, kvw), F32),
             pltpu.VMEM((n_dev - 1, group, kvw // nx), F32),
             pltpu.VMEM((nz, group, kvw // nx), F32),
-            pltpu.VMEM((group, kvw // nx), F32),
             pltpu.VMEM((rank, kvw), F32),
             pltpu.VMEM((rank, 2 * rank), F32),
             dma((3, pieces)),
@@ -350,10 +369,23 @@
             dma((6,)),
         ],
         compiler_params=pltpu.CompilerParams(
-            collective_id=0, has_side_effects=True, vmem_limit_bytes=40 * 2**20
+            collective_id=0, has_side_effects=True, vmem_limit_bytes=36 * 2**20
         ),
         name="powersgd",
-    )(inputs, cotangent, errors, previous_q.T)
+    )(*[pltpu.with_memory_space_constraint(a, pltpu.HBM) for a in (inputs, cotangent, errors, previous_q.T)])
+    new_errors, p_hat, q_mean = pl.pallas_call(
+        finish,
+        out_shape=(
+            jax.ShapeDtypeStruct((width, kvw), BF16),
+            jax.ShapeDtypeStruct((rank, width), F32),
+            jax.ShapeDtypeStruct((rank, kvw), F32),
+        ),
+        in_specs=[vmem, vmem, vmem, vmem],
+        out_specs=(hbm, hbm, hbm),
+        scratch_shapes=[pltpu.VMEM((pieces, w, kvw), BF16), dma((pieces,)), dma((2,))],
+        compiler_params=pltpu.CompilerParams(vmem_limit_bytes=24 * 2**20),
+        name="new_errors",
+    )(merged, left_parts, p_hat, q_mean)
     return new_errors[None], p_hat.T, q_mean.T
 
 

time: 62 us -> 51.8 us (0.84)
  local copies, waits for them, and re-layouts: 8.92 us -> 0 us
  Pallas kernels: 52.2 us -> 51.1 us
    unnamed x11 -> x0, local copies, waits for them, and re-layouts: 8.92 us -> none
    pallas_call x1, Pallas kernels: 52.2 us -> 49.1 us  [step(): pl.pallas_call(functools.partial(kernel, nx, ny, nz), out_shape=(jax.Shap...]
    pallas_call x0 -> x1, Pallas kernels: none -> 2.05 us  [step(): pl.pallas_call(finish, out_shape=(jax.ShapeDtypeStruct((width, kvw), BF16...]
where the time goes in v2:
time: 51.8 us
  Pallas kernels  51.1 us (99%)
  between operations  0.64 us (1%)
    pallas_call x1, Pallas kernels, step(): pl.pallas_call(functools.partial(kernel, nx, ny, nz), out_shape=(jax.Shap...  49.1 us
    pallas_call x1, Pallas kernels, step(): pl.pallas_call(finish, out_shape=(jax.ShapeDtypeStruct((width, kvw), BF16...  2.05 us

profile of v2, /device:TPU:1, one launch (start us, length us, event | category | flops | bytes accessed | tf_op | source)
XLA Modules:
  0.0 51.8 jit_solution(16704532543305179956)
XLA Ops:
  0.6 49.1 %powersgd.1 = (f32[8,384,512]{2,1,0:T(8,128)S(1)}, bf16[8,384,192]{2,1,0:T(8,128)(2,1)S(1)}, f32[64,3072]{1,0:T(8,128)S(1)}, f32[64,512]{1,0:T(8,128)S(1)}) custom-call(bf16[512,3072]{1,0:T(8,128)(2,1)} %x_hbm.1, bf16[512,512]{1,0:T(8,128)(2,1)} %y_hbm.1, bf16[1,3072,512]{2,1,0:T(8,128)(2,1)} %e_hbm.1, f32[64,512]{1,0:T(8,128)} %bitcast.4), custom_call_target="tpu_custom_call" | custom-call | tf_op jit(solution)/shard_map/powersgd/pallas_call | solution.py:329
  49.7 2.0 %new_errors.1 = (bf16[3072,512]{1,0:T(8,128)(2,1)}, f32[64,3072]{1,0:T(8,128)}, f32[64,512]{1,0:T(8,128)}) custom-call(f32[8,384,512]{2,1,0:T(8,128)S(1)} %get-tuple-element.10.merged, bf16[8,384,192]{2,1,0:T(8,128)(2,1)S(1)} %get-tuple-element.11.left_parts, f32[64,3072]{1,0:T(8,128)S(1)} %get-tuple-element.12.phat_ref, ...), custom_call_target="tpu_custom_call" | custom-call | tf_op jit(solution)/shard_map/new_errors/pallas_call | solution.py:376

commit v3 on v2

--- a/solution.py
+++ b/solution.py
@@ -34,9 +34,9 @@
     x_hbm, y_hbm, e_hbm, qt_hbm,
     merged, left_parts, phat_ref, qmean_ref,
     xv, ev, yv, qt_ref, m_high, m_low, base,
-    part, core_in, chip_sum, plane_in, z_in, full,
+    part, core_in, chip_sum, line_in, line_sum, cell_in, z_in, full,
     g_own, g_in, gz_in, g_full, aug,
-    load_sem, core_send, core_recv, rs_send, rs_recv, z_send, z_recv,
+    load_sem, core_send, core_recv, rs_send, rs_recv, cell_send, cell_recv, z_send, z_recv,
     ag_send, ag_recv, fw_send, fw_recv, g_sem,
 ):
     subs = SUBS
@@ -121,14 +121,21 @@
         s, step = order[i]
         core_copy(i).wait_recv()
         chip_sum[i] = part[i, pl.ds(c * ny, ny)] + core_in[i]
-        for dy in far_first(ny):
-            if step == 0 and dy == 0:
-                continue
-            slot = ((nx - step) % nx) * ny + (ny - dy) % ny - 1
-            yy = away(y, dy, ny)
-            remote(
-                chip_sum.at[i, yy], plane_in.at[s, slot], rs_send, rs_recv.at[s], at(away(x, step, nx), yy, c)
-            ).start()
+        if step:
+            @pl.when(c == 0)
+            def _():
+                slot = (nx - step) % nx - 1
+                to = at(away(x, step, nx), y, c)
+                remote(chip_sum.at[i], line_in.at[s, slot], rs_send, rs_recv.at[s], to).start()
+        else:
+            @pl.when(c == 1)
+            def _():
+                for dy in far_first(ny)[:-1]:
+                    yy = away(y, dy, ny)
+                    remote(
+                        chip_sum.at[pl.ds(s * nx, nx), yy], line_in.at[s, (ny - dy) % ny - 1],
+                        rs_send, rs_recv.at[s], at(x, yy, c),
+                    ).start()
 
     def merge_piece(i):
         s, step = order[i]
@@ -152,11 +159,35 @@
 
     own = [i for i in range(pieces) if order[i][1] == 0]
 
+    def line(s):
+        wait_bytes(line_in.at[s], rs_recv.at[s])
+        total = line_in[s, 0]
+        for k in range(1, nx - 1):
+            total = total + line_in[s, k]
+
+        @pl.when(c == 0)
+        def _():
+            line_sum[s] = total + chip_sum[own[s]]
+            for dy in far_first(ny)[:-1]:
+                yy = away(y, dy, ny)
+                remote(
+                    line_sum.at[s, yy], cell_in.at[s, (ny - dy) % ny - 1], cell_send, cell_recv.at[s], at(x, yy, c)
+                ).start()
+
+        @pl.when(c == 1)
+        def _():
+            line_sum[s] = total + chip_sum[pl.ds(s * nx, nx), y]
+            for t, step in enumerate(far_first(nx)[:-1]):
+                to = at(away(x, step, nx), y, c)
+                remote(
+                    line_sum.at[s, t], cell_in.at[s, (nx - step) % nx - 1], cell_send, cell_recv.at[s], to
+                ).start()
+
     def exchange(s):
-        wait_bytes(plane_in.at[s], rs_recv.at[s])
-        total = chip_sum[own[s], y]
-        for slot in range(nx * ny - 1):
-            total = total + plane_in[s, slot]
+        wait_bytes(cell_in.at[s], cell_recv.at[s])
+        total = line_sum[s, (1 - c) * y + c * (nx - 1)]
+        for k in range(nx - 1):
+            total = total + cell_in[s, k]
         z_in[s, z] = total
         for k in far_first(nz)[:-1]:
             remote(z_in.at[s, z], z_in.at[s, z], z_send, z_recv.at[s], (away(z, k, nz), d)).start()
@@ -176,6 +207,8 @@
                 at(away(x, dx, nx), away(y, dy, ny), c),
             ).start()
 
+    for s in range(subs):
+        line(s)
     rest = list(range(early, pieces))
     for s in range(subs):
         exchange(s)
@@ -286,9 +319,10 @@
 
     for i in range(pieces):
         core_copy(i).wait_send()
-    wait_bytes(plane_in, rs_send)
+    wait_bytes(line_in, rs_send)
+    wait_bytes(cell_in, cell_send)
     wait_bytes(z_in.at[:, pl.ds(0, nz - 1)], z_send)
-    wait_bytes(plane_in, ag_send)
+    wait_bytes(part.at[pl.ds(0, 5), pl.ds(0, 6)], ag_send)
     wait_bytes(core_in, fw_send)
     wait_bytes(g_in, g_sem.at[0])
     wait_bytes(gz_in.at[pl.ds(0, nz - 1)], g_sem.at[2])
@@ -347,7 +381,9 @@
             pltpu.VMEM((pieces, 2 * ny, group, w), F32),
             pltpu.VMEM((pieces, ny, group, w), F32),
             pltpu.VMEM((pieces, ny, group, w), F32),
-            pltpu.VMEM((subs, nx * ny - 1, group, w), F32),
+            pltpu.VMEM((subs, nx - 1, ny, group, w), F32),
+            pltpu.VMEM((subs, ny, group, w), F32),
+            pltpu.VMEM((subs, nx - 1, group, w), F32),
             pltpu.VMEM((subs, nz, group, w), F32),
             pltpu.VMEM((pieces, 2 * ny, group, w), F32),
             pltpu.VMEM((rank, kvw), F32),
@@ -358,6 +394,8 @@
             dma((3, pieces)),
             dma((pieces,)),
             dma((pieces,)),
+            dma(()),
+            dma((subs,)),
             dma(()),
             dma((subs,)),
             dma(()),

time: 51.8 us -> 53.2 us (1.027)
  Pallas kernels: 51.1 us -> 52.5 us
    pallas_call x1, Pallas kernels: 49.1 us -> 50.4 us  [step(): pl.pallas_call(functools.partial(kernel, nx, ny, nz), out_shape=(jax.Shap...]
where the time goes in v3:
time: 53.2 us; the launch traced here: 53.1 us
  Pallas kernels  52.5 us (99%)
  between operations  0.64 us (1%)
    pallas_call x1, Pallas kernels, step(): pl.pallas_call(functools.partial(kernel, nx, ny, nz), out_shape=(jax.Shap...  50.4 us
    pallas_call x1, Pallas kernels, step(): pl.pallas_call(finish, out_shape=(jax.ShapeDtypeStruct((width, kvw), BF16...  2.05 us

profile of v3, /device:TPU:1, one launch (start us, length us, event | category | flops | bytes accessed | tf_op | source)
XLA Modules:
  0.0 53.1 jit_solution(6095274568954119925)
XLA Ops:
  0.6 50.4 %powersgd.1 = (f32[8,384,512]{2,1,0:T(8,128)S(1)}, bf16[8,384,192]{2,1,0:T(8,128)(2,1)S(1)}, f32[64,3072]{1,0:T(8,128)S(1)}, f32[64,512]{1,0:T(8,128)S(1)}) custom-call(bf16[512,3072]{1,0:T(8,128)(2,1)} %x_hbm.1, bf16[512,512]{1,0:T(8,128)(2,1)} %y_hbm.1, bf16[1,3072,512]{2,1,0:T(8,128)(2,1)} %e_hbm.1, f32[64,512]{1,0:T(8,128)} %bitcast.4), custom_call_target="tpu_custom_call" | custom-call | tf_op jit(solution)/shard_map/powersgd/pallas_call | solution.py:363
  51.1 2.0 %new_errors.1 = (bf16[3072,512]{1,0:T(8,128)(2,1)}, f32[64,3072]{1,0:T(8,128)}, f32[64,512]{1,0:T(8,128)}) custom-call(f32[8,384,512]{2,1,0:T(8,128)S(1)} %get-tuple-element.10.merged, bf16[8,384,192]{2,1,0:T(8,128)(2,1)S(1)} %get-tuple-element.11.left_parts, f32[64,3072]{1,0:T(8,128)S(1)} %get-tuple-element.12.phat_ref, ...), custom_call_target="tpu_custom_call" | custom-call | tf_op jit(solution)/shard_map/new_errors/pallas_call | solution.py:414

commit v4 on v2

--- a/solution.py
+++ b/solution.py
@@ -176,11 +176,10 @@
                 at(away(x, dx, nx), away(y, dy, ny), c),
             ).start()
 
-    rest = list(range(early, pieces))
+    for i in range(early, pieces):
+        merge_piece(i)
     for s in range(subs):
         exchange(s)
-        for i in rest[s * len(rest) // subs:(s + 1) * len(rest) // subs]:
-            merge_piece(i)
     for s in range(subs):
         spread(s)
 

time: 51.8 us -> 51.9 us (level)
  no operation moved by 1% of the time
where the time goes in v4:
time: 51.9 us; the launch traced here: 51.8 us
  Pallas kernels  51.2 us (99%)
  between operations  0.64 us (1%)
    pallas_call x1, Pallas kernels, step(): pl.pallas_call(functools.partial(kernel, nx, ny, nz), out_shape=(jax.Shap...  49.1 us
    pallas_call x1, Pallas kernels, step(): pl.pallas_call(finish, out_shape=(jax.ShapeDtypeStruct((width, kvw), BF16...  2.05 us

profile of v4, /device:TPU:1, one launch (start us, length us, event | category | flops | bytes accessed | tf_op | source)
XLA Modules:
  0.0 51.8 jit_solution(5545698141119579372)
XLA Ops:
  0.6 49.1 %powersgd.1 = (f32[8,384,512]{2,1,0:T(8,128)S(1)}, bf16[8,384,192]{2,1,0:T(8,128)(2,1)S(1)}, f32[64,3072]{1,0:T(8,128)S(1)}, f32[64,512]{1,0:T(8,128)S(1)}) custom-call(bf16[512,3072]{1,0:T(8,128)(2,1)} %x_hbm.1, bf16[512,512]{1,0:T(8,128)(2,1)} %y_hbm.1, bf16[1,3072,512]{2,1,0:T(8,128)(2,1)} %e_hbm.1, f32[64,512]{1,0:T(8,128)} %bitcast.4), custom_call_target="tpu_custom_call" | custom-call | tf_op jit(solution)/shard_map/powersgd/pallas_call | solution.py:328
  49.8 2.0 %new_errors.1 = (bf16[3072,512]{1,0:T(8,128)(2,1)}, f32[64,3072]{1,0:T(8,128)}, f32[64,512]{1,0:T(8,128)}) custom-call(f32[8,384,512]{2,1,0:T(8,128)S(1)} %get-tuple-element.10.merged, bf16[8,384,192]{2,1,0:T(8,128)(2,1)S(1)} %get-tuple-element.11.left_parts, f32[64,3072]{1,0:T(8,128)S(1)} %get-tuple-element.12.phat_ref, ...), custom_call_target="tpu_custom_call" | custom-call | tf_op jit(solution)/shard_map/new_errors/pallas_call | solution.py:375
